TPU v7x, 32 devices: a whole 2x2x4 slice. The times are simulated.
32 devices in a mesh: strip: 2 (over x), row: 16 (over z, y, core).
Axes of the slice: x: 2, y: 2, z: 4, core: 2. Of those that a mesh axis runs over, the one named last changes fastest.
Arguments:
- mask: float32 [512, 256], P(('strip', 'row')), parts along dimension 0, may hold values from 0 to 1
- target: float32 [512, 256], P(('strip', 'row')), parts along dimension 0, may hold values from 0 to 1
- kernels: bfloat16 [9, 24, 17, 17], replicated, may hold values from -0.375 to 0.375
- corner_weights: float32 [9, 12], replicated, may hold values from 0.03 to 0.3
- hotspots: int32 [32, 5], P('strip'), parts along dimension 0, may hold values from 0 to 8, as said below
- counts: int32 [32], P('strip'), parts along dimension 0, may hold values from 1 to 5, as said below
Outputs:
- updated_mask: float32 [512, 256], P(('strip', 'row')), parts along dimension 0
There are 2 independent parts, one for each index of `strip`. A program takes and returns all parts, laid end to end along the dimension named above; an argument that names none is the same for every part. Nothing has to cross between parts.
Inputs may be any that keep to these rules, and one draw needn't show every extreme that they name: `hotspots`: each row names 5 distinct corners. `counts`: some tile has 5 in every draw; tiles t and t xor (8) together use at most 6 corners, and some such pair reaches it in every draw.
All inputs are finite; a program needn't handle non-finite values.
Results may differ from a plain program's by a relative error of at most 0.0062.
Values may be sent and summed in bfloat16 or wider, within the bound.
A program may use at most 64 MiB of HBM per device.

v0:
```python
import functools

import jax
import jax.numpy as jnp
from jax import lax
from jax.experimental import pallas as pl
from jax.experimental.pallas import tpu as pltpu
from jax.sharding import PartitionSpec as P

ITERS = 2
STEEPNESS = 4.0
THRESHOLD = 0.8
STEP_RATE = 1.0
LANES = 128
MESH = pl.DeviceIdType.MESH


def cdiv(a, b):
    return -(-a // b)


def round_up(a, b):
    return cdiv(a, b) * b


class Plan:
    def __init__(self, rows, width, channels, side, slots):
        self.rows, self.width, self.channels = rows, width, channels
        self.side, self.slots = side, slots
        self.radius = side // 2
        self.groups = rows // self.radius
        self.ext = rows + 2 * self.radius
        self.window = 3 * self.radius
        self.per = LANES // self.window
        self.stretches = cdiv(side, self.per)
        self.depth = self.stretches * LANES
        self.used = round_up(self.offset(side - 1) + self.window, 16)
        self.slot_rows = channels * self.radius
        self.mix = round_up(slots * self.slot_rows, 256)

    def offset(self, b):
        return (b // self.per) * LANES + (b % self.per) * self.window


def shifted(value, by):
    width = value.shape[1]
    if by == 0:
        return value
    moved = pltpu.roll(value, by % width, 1)
    column = lax.broadcasted_iota(jnp.int32, value.shape, 1)
    keep = column >= by if by > 0 else column < width + by
    return jnp.where(keep, moved, 0.0)


def kernel(p, devices, hot_ref, count_ref, weight_ref, mask_ref, target_ref, base_ref, out_ref,
           big, big_t, patches, source, field, total, halo, got, send_sem, recv_sem):
    me = lax.axis_index("row")
    r = p.radius
    has_up, has_down = me > 0, me < devices - 1
    kinds = weight_ref.shape[1]

    barrier = pltpu.get_barrier_semaphore()

    @pl.when(has_up)
    def _():
        pl.semaphore_signal(barrier, inc=1, device_id={"row": me - 1}, device_id_type=MESH)

    @pl.when(has_down)
    def _():
        pl.semaphore_signal(barrier, inc=1, device_id={"row": me + 1}, device_id_type=MESH)

    def copies(stage, up_src, down_src, above, below):
        up = pltpu.make_async_remote_copy(
            src_ref=up_src, dst_ref=below, send_sem=send_sem.at[stage, 0],
            recv_sem=recv_sem.at[stage, 0], device_id={"row": me - 1}, device_id_type=MESH)
        down = pltpu.make_async_remote_copy(
            src_ref=down_src, dst_ref=above, send_sem=send_sem.at[stage, 1],
            recv_sem=recv_sem.at[stage, 1], device_id={"row": me + 1}, device_id_type=MESH)
        return up, down

    def start(pair):
        up, down = pair

        @pl.when(has_up)
        def _():
            up.start()

        @pl.when(has_down)
        def _():
            down.start()

    def finish(pair):
        up, down = pair

        @pl.when(has_up)
        def _():
            up.wait_send()
            down.wait_recv()

        @pl.when(has_down)
        def _():
            down.wait_send()
            up.wait_recv()

    @pl.when(jnp.logical_not(has_up))
    def _():
        halo[0] = jnp.zeros(halo.shape[1:], halo.dtype)
        for step in range(ITERS):
            got[step, 0] = jnp.zeros(got.shape[2:], got.dtype)

    @pl.when(jnp.logical_not(has_down))
    def _():
        halo[1] = jnp.zeros(halo.shape[1:], halo.dtype)
        for step in range(ITERS):
            got[step, 1] = jnp.zeros(got.shape[2:], got.dtype)

    inner = has_up & has_down

    @pl.when(inner)
    def _():
        pl.semaphore_wait(barrier, 2)

    @pl.when(jnp.logical_not(inner))
    def _():
        pl.semaphore_wait(barrier, 1)

    first = copies(0, mask_ref.at[pl.ds(0, r)], mask_ref.at[pl.ds(p.rows - r, r)],
                   halo.at[0], halo.at[1])
    start(first)

    corners = [hot_ref[me, s] for s in range(p.slots)]
    count = count_ref[me]
    for s in range(p.slots):
        base = base_ref[corners[s]]
        for q in range(p.stretches):
            part = base[:, q * LANES : (q + 1) * LANES]
            wide = jnp.broadcast_to(part[:, None, :], (p.channels, r, LANES))
            turned = pltpu.roll(wide, 0, 2, stride=1, stride_axis=1)
            flat = turned.reshape(p.slot_rows, LANES)
            big[pl.ds(s * p.slot_rows, p.slot_rows), pl.ds(q * LANES, LANES)] = flat
    rest = p.mix - p.slots * p.slot_rows
    if rest:
        big[pl.ds(p.slots * p.slot_rows, rest), :] = jnp.zeros((rest, p.depth), jnp.float32)
        source[pl.ds(p.slots * p.slot_rows, rest), :] = jnp.zeros((rest, source.shape[1]), jnp.bfloat16)
    for q in range(p.mix // 256):
        big_t[:, pl.ds(q * 256, 256)] = big[pl.ds(q * 256, 256), :].T.astype(jnp.bfloat16)

    target = jnp.concatenate([target_ref[pl.ds(g * r, r), :] for g in range(p.groups)], axis=1)
    finish(first)
    field[pl.ds(0, r), :] = halo[0]
    field[pl.ds(r, p.rows), :] = mask_ref[...]
    field[pl.ds(r + p.rows, r), :] = halo[1]

    for step in range(ITERS):
        low = field[...].astype(jnp.bfloat16).astype(jnp.float32)
        for q in range(p.stretches):
            blocks = []
            for b in range(q * p.per, min((q + 1) * p.per, p.side)):
                moved = shifted(low, r - b)
                blocks.append(jnp.concatenate(
                    [moved[g * r : g * r + p.window] for g in range(p.groups)], axis=1))
            gap = LANES - len(blocks) * p.window
            blocks.append(jnp.zeros((gap, p.groups * p.width), jnp.float32))
            patches[pl.ds(q * LANES, LANES), :] = jnp.concatenate(blocks, axis=0).astype(jnp.bfloat16)

        for s in range(p.slots):
            rows = pl.ds(s * p.slot_rows, p.slot_rows)
            image = jnp.dot(big[rows, :].astype(jnp.bfloat16), patches[...],
                            preferred_element_type=jnp.float32)
            image = image.reshape(p.channels, r, p.groups * p.width)
            weights = [weight_ref[corners[s], k] for k in range(kinds)]
            intensity = jnp.zeros((r, p.groups * p.width), jnp.float32)
            for j in range(p.channels):
                intensity = intensity + weights[j % kinds] * (image[j] * image[j])
            resist = jax.nn.sigmoid(STEEPNESS * (intensity - THRESHOLD))
            slope = 2.0 * (resist - target) * STEEPNESS * resist * (1.0 - resist)
            slope = jnp.where(s < count, slope, 0.0)
            scaled = [(2.0 * weights[k]) * slope for k in range(kinds)]
            sent = jnp.stack([scaled[j % kinds] * image[j] for j in range(p.channels)])
            source[rows, :] = sent.reshape(p.slot_rows, p.groups * p.width).astype(jnp.bfloat16)

        spread = jnp.dot(big_t[pl.ds(0, p.used), :], source[...], preferred_element_type=jnp.float32)
        sums = jnp.zeros((p.ext, p.width), jnp.float32)
        for b in range(p.side):
            block = spread[p.offset(b) : p.offset(b) + p.window]
            joined = 0.0
            for g in range(p.groups):
                piece = block[:, g * p.width : (g + 1) * p.width]
                parts = []
                if g:
                    parts.append(jnp.zeros((g * r, p.width), jnp.float32))
                parts.append(piece)
                tail = p.ext - p.window - g * r
                if tail:
                    parts.append(jnp.zeros((tail, p.width), jnp.float32))
                joined = joined + jnp.concatenate(parts, axis=0)
            sums = sums + shifted(joined, b - r)
        total[step] = sums

        half = p.ext // 2
        if step < ITERS - 1:
            pair = copies(step + 1, total.at[step, pl.ds(0, half)], total.at[step, pl.ds(half, half)],
                          got.at[step, 0], got.at[step, 1])
            start(pair)
            finish(pair)
            gradient = sums + jnp.concatenate([got[step, 0], got[step, 1]], axis=0)
            after = field[...] - STEP_RATE * gradient
            row = lax.broadcasted_iota(jnp.int32, after.shape, 0)
            inside = ((row >= r) | has_up) & ((row < p.ext - r) | has_down)
            field[...] = jnp.where(inside, after, 0.0)
        else:
            pair = copies(step + 1, total.at[step, pl.ds(0, r)], total.at[step, pl.ds(p.ext - r, r)],
                          got.at[step, 0, pl.ds(half - r, r)], got.at[step, 1, pl.ds(0, r)])
            start(pair)
            finish(pair)
            outer = jnp.concatenate([got[step, 0, pl.ds(half - r, r)], got[step, 1, pl.ds(0, r)]], axis=0)
            own = sums[r : r + p.rows]
            out_ref[...] = field[pl.ds(r, p.rows), :] - STEP_RATE * (own + outer)


def laid_out(kernels, p):
    corners, channels, side, _ = kernels.shape
    value = jnp.swapaxes(kernels, 2, 3).astype(jnp.float32)
    value = jnp.pad(value, ((0, 0), (0, 0), (0, p.stretches * p.per - side), (0, p.window - side)))
    value = value.reshape(corners, channels, p.stretches, p.per * p.window)
    value = jnp.pad(value, ((0, 0), (0, 0), (0, 0), (0, LANES - p.per * p.window)))
    return value.reshape(corners, channels, p.depth)


def body(devices, mask, target, kernels, corner_weights, hotspots, counts):
    rows, width = mask.shape
    p = Plan(rows, width, kernels.shape[1], kernels.shape[-1], hotspots.shape[1])
    assert rows == 2 * p.radius and p.radius == 8
    base = laid_out(kernels, p)
    smem = pl.BlockSpec(memory_space=pltpu.SMEM)
    vmem = pl.BlockSpec(memory_space=pltpu.VMEM)
    wide = p.groups * width
    return pl.pallas_call(
        functools.partial(kernel, p, devices),
        out_shape=jax.ShapeDtypeStruct((rows, width), jnp.float32),
        in_specs=[smem, smem, smem, vmem, vmem, vmem],
        out_specs=vmem,
        scratch_shapes=[
            pltpu.VMEM((p.mix, p.depth), jnp.float32),
            pltpu.VMEM((p.depth, p.mix), jnp.bfloat16),
            pltpu.VMEM((p.depth, wide), jnp.bfloat16),
            pltpu.VMEM((p.mix, wide), jnp.bfloat16),
            pltpu.VMEM((p.ext, width), jnp.float32),
            pltpu.VMEM((ITERS, p.ext, width), jnp.float32),
            pltpu.VMEM((2, p.radius, width), jnp.float32),
            pltpu.VMEM((ITERS, 2, p.ext // 2, width), jnp.float32),
            pltpu.SemaphoreType.DMA((ITERS + 1, 2)),
            pltpu.SemaphoreType.DMA((ITERS + 1, 2)),
        ],
        compiler_params=pltpu.CompilerParams(collective_id=0, has_side_effects=True),
        name="litho",
    )(hotspots, counts, corner_weights, mask, target, base)


def solution(mesh):
    placed = (
        P(("strip", "row"), None),
        P(("strip", "row"), None),
        P(),
        P(),
        P("strip", None),
        P("strip"),
    )
    return jax.shard_map(
        functools.partial(body, mesh.shape["row"]), mesh=mesh, in_specs=placed,
        out_specs=P(("strip", "row"), None), check_vma=False
    )
```

profile of v0, /device:TPU:7, one launch (start us, length us, event | category | flops | bytes accessed | tf_op | source)
XLA Modules:
  0.0 21.5 jit_solution(16617912421020481512)
XLA Ops:
  0.0 3.4 %copy.10 = bf16[9,24,17,17]{3,2,1,0:T(8,128)(2,1)S(1)} copy(bf16[9,24,17,17]{2,1,3,0:T(8,128)(2,1)} %bitcast.1) | data formatting | bytes 249696
  3.4 0.3 %pad.10.clone = bf16[9,24,20,24]{3,2,1,0:T(8,128)(2,1)S(1)} pad(bf16[9,24,17,17]{3,2,1,0:T(8,128)(2,1)S(1)} %copy.10, bf16[]{:T(256)} %constant.3.clone.1), padding=0_0x0_0x0_3x0_7 | pad | bytes 332210 | tf_op jit(solution)/shard_map/jit(_pad)/pad | solution.py:224
  3.7 0.0 copy-start
  3.7 0.7 %reshape.9 = bf16[9,24,4,120]{3,2,1,0:T(4,128)(2,1)S(1)} reshape(bf16[9,24,20,24]{3,2,1,0:T(8,128)(2,1)S(1)} %pad.10.clone) | data formatting | bytes 414720 | tf_op jit(solution)/shard_map/reshape | solution.py:225
  4.5 0.1 pad_convert_fusion
  4.6 0.9 %reshape.13.base_ref = f32[9,24,512]{2,1,0:T(8,128)} reshape(f32[9,24,4,128]{3,2,1,0:T(4,128)S(1)} %pad_convert_fusion) | data formatting | bytes 884736 | tf_op jit(solution)/shard_map/reshape | solution.py:227
  5.5 0.0 copy-done
  5.5 0.7 %copy.9.hot_ref = s32[16,5]{1,0:T(8,128)} copy(s32[16,5]{0,1:T(8,128)S(1)} %copy-done) | data formatting | bytes 640 | tf_op args[4]
  6.2 13.9 %litho.1 = f32[16,256]{1,0:T(8,128)} custom-call(s32[16,5]{1,0:T(8,128)} %copy.9.hot_ref, s32[16]{0:T(128)} %count_ref.1, f32[9,12]{1,0:T(8,128)} %weight_ref.1, f32[16,256]{1,0:T(8,128)} %mask_ref.1, f32[16,256]{1,0:T(8,128)} %target_ref.1, f32[9,24,512]{2,1,0:T(8,128)} %reshape.13.base_ref), custom_call_target="tpu_custom_call" | custom-call | tf_op jit(solution)/shard_map/litho/pallas_call | solution.py:238
  20.2 1.3 %copy.12 = f32[16,256]{1,0:T(8,128)} copy(f32[16,256]{1,0:T(8,128)} %litho.1) | data formatting | bytes 32768
Async XLA Ops:
  3.7 1.8 %copy-start = (s32[16,5]{0,1:T(8,128)S(1)}, s32[16,5]{0,1:T(8,128)}, u32[]{:S(2)}) copy-start(s32[16,5]{0,1:T(8,128)} %param.10) | copy-start | bytes 964
where the time goes:
time: 21.7 us; the launch traced here: 21.5 us
  Pallas kernels  13.9 us (64%)
  local copies, waits for them, and re-layouts  7.38 us (34%)
    pallas_call x1, Pallas kernels, body(): pl.pallas_call(functools.partial(kernel, p, devices), out_shape=jax.Shape...  13.9 us
    unnamed x5, local copies, waits for them, and re-layouts  5.4 us
    reshape x1, local copies, waits for them, and re-layouts, laid_out(): return value.reshape(corners, channels, p.depth)  0.94 us
    reshape x1, local copies, waits for them, and re-layouts, laid_out(): value = value.reshape(corners, channels, p.stretches, p.per * p.window)  0.73 us

commit v1 on v0

--- a/solution.py
+++ b/solution.py
@@ -34,7 +34,9 @@
         self.per = LANES // self.window
         self.stretches = cdiv(side, self.per)
         self.depth = self.stretches * LANES
-        self.used = round_up(self.offset(side - 1) + self.window, 16)
+        self.block = round_up(side * self.radius, 16)
+        self.lane_step = 32
+        self.packed = cdiv(side * self.lane_step, LANES) * LANES
         self.slot_rows = channels * self.radius
         self.mix = round_up(slots * self.slot_rows, 256)
 
@@ -52,13 +54,16 @@
     return jnp.where(keep, moved, 0.0)
 
 
-def kernel(p, devices, hot_ref, count_ref, weight_ref, mask_ref, target_ref, base_ref, out_ref,
-           big, big_t, patches, source, field, total, halo, got, send_sem, recv_sem):
+def kernel(p, devices, hot_ref, count_ref, weight_ref, mask_ref, target_ref, taps_hbm, out_ref,
+           taps, pack, big, big_low, big_t, patches, source, field, total, halo, got,
+           load_sem, send_sem, recv_sem):
     me = lax.axis_index("row")
     r = p.radius
     has_up, has_down = me > 0, me < devices - 1
     kinds = weight_ref.shape[1]
 
+    load = pltpu.make_async_copy(taps_hbm, taps, load_sem)
+    load.start()
     barrier = pltpu.get_barrier_semaphore()
 
     @pl.when(has_up)
@@ -114,6 +119,27 @@
         for step in range(ITERS):
             got[step, 1] = jnp.zeros(got.shape[2:], got.dtype)
 
+    shape = (p.packed, p.depth)
+    spot = lax.broadcasted_iota(jnp.int32, (1, p.depth), 1)
+    inside = spot & (LANES - 1)
+    nth = jnp.zeros_like(spot)
+    for k in range(1, p.per + 1):
+        nth = nth + (inside >= k * p.window).astype(jnp.int32)
+    tap_row = inside - nth * p.window
+    tap_col = (spot // LANES) * p.per + nth
+    valid = (nth < p.per) & (tap_row < p.side) & (tap_col < p.side)
+    wanted = jnp.where(valid, tap_row * p.lane_step + tap_col, -1)
+    place = (lax.broadcasted_iota(jnp.int32, shape, 0) == wanted).astype(jnp.float32).astype(jnp.bfloat16)
+
+    corners = [hot_ref[s, me] for s in range(p.slots)]
+    count = count_ref[me]
+    pack[...] = jnp.zeros(pack.shape, jnp.float32)
+    load.wait()
+    for s in range(p.slots):
+        for a in range(p.side):
+            pack[pl.ds(s * p.channels, p.channels), pl.ds(a * p.lane_step, p.side)] = (
+                taps[corners[s], a].astype(jnp.float32))
+
     inner = has_up & has_down
 
     @pl.when(inner)
@@ -128,22 +154,31 @@
                    halo.at[0], halo.at[1])
     start(first)
 
-    corners = [hot_ref[me, s] for s in range(p.slots)]
-    count = count_ref[me]
+    base = jnp.dot(pack[...].astype(jnp.bfloat16), place, preferred_element_type=jnp.float32)
     for s in range(p.slots):
-        base = base_ref[corners[s]]
         for q in range(p.stretches):
-            part = base[:, q * LANES : (q + 1) * LANES]
+            part = base[s * p.channels : (s + 1) * p.channels, q * LANES : (q + 1) * LANES]
             wide = jnp.broadcast_to(part[:, None, :], (p.channels, r, LANES))
             turned = pltpu.roll(wide, 0, 2, stride=1, stride_axis=1)
             flat = turned.reshape(p.slot_rows, LANES)
-            big[pl.ds(s * p.slot_rows, p.slot_rows), pl.ds(q * LANES, LANES)] = flat
+            where = (pl.ds(s * p.slot_rows, p.slot_rows), pl.ds(q * LANES, LANES))
+            big[where] = flat
+            big_low[where] = flat.astype(jnp.bfloat16)
     rest = p.mix - p.slots * p.slot_rows
     if rest:
         big[pl.ds(p.slots * p.slot_rows, rest), :] = jnp.zeros((rest, p.depth), jnp.float32)
         source[pl.ds(p.slots * p.slot_rows, rest), :] = jnp.zeros((rest, source.shape[1]), jnp.bfloat16)
     for q in range(p.mix // 256):
-        big_t[:, pl.ds(q * 256, 256)] = big[pl.ds(q * 256, 256), :].T.astype(jnp.bfloat16)
+        turned = big[pl.ds(q * 256, 256), :].T
+        rows = []
+        for third in range(p.window // r):
+            for b in range(p.side):
+                at = p.offset(b) + third * r
+                rows.append(turned[at : at + r])
+            spare = p.block - p.side * r
+            if spare:
+                rows.append(jnp.zeros((spare, 256), jnp.float32))
+        big_t[:, pl.ds(q * 256, 256)] = jnp.concatenate(rows, axis=0).astype(jnp.bfloat16)
 
     target = jnp.concatenate([target_ref[pl.ds(g * r, r), :] for g in range(p.groups)], axis=1)
     finish(first)
@@ -165,7 +200,7 @@
 
         for s in range(p.slots):
             rows = pl.ds(s * p.slot_rows, p.slot_rows)
-            image = jnp.dot(big[rows, :].astype(jnp.bfloat16), patches[...],
+            image = jnp.dot(big_low[rows, :], patches[...],
                             preferred_element_type=jnp.float32)
             image = image.reshape(p.channels, r, p.groups * p.width)
             weights = [weight_ref[corners[s], k] for k in range(kinds)]
@@ -179,82 +214,74 @@
             sent = jnp.stack([scaled[j % kinds] * image[j] for j in range(p.channels)])
             source[rows, :] = sent.reshape(p.slot_rows, p.groups * p.width).astype(jnp.bfloat16)
 
-        spread = jnp.dot(big_t[pl.ds(0, p.used), :], source[...], preferred_element_type=jnp.float32)
-        sums = jnp.zeros((p.ext, p.width), jnp.float32)
-        for b in range(p.side):
-            block = spread[p.offset(b) : p.offset(b) + p.window]
-            joined = 0.0
-            for g in range(p.groups):
-                piece = block[:, g * p.width : (g + 1) * p.width]
-                parts = []
-                if g:
-                    parts.append(jnp.zeros((g * r, p.width), jnp.float32))
-                parts.append(piece)
-                tail = p.ext - p.window - g * r
-                if tail:
-                    parts.append(jnp.zeros((tail, p.width), jnp.float32))
-                joined = joined + jnp.concatenate(parts, axis=0)
-            sums = sums + shifted(joined, b - r)
-        total[step] = sums
-
-        half = p.ext // 2
+        def spread(third, thirds, group):
+            return jnp.dot(big_t[pl.ds(third * p.block, thirds * p.block), :],
+                           source[:, pl.ds(group * p.width, p.width)], preferred_element_type=jnp.float32)
+
+        def summed(value, thirds):
+            sums = jnp.zeros((thirds * r, p.width), jnp.float32)
+            for b in range(p.side):
+                rows = [value[k * p.block + b * r : k * p.block + (b + 1) * r] for k in range(thirds)]
+                sums = sums + shifted(rows[0] if thirds == 1 else jnp.concatenate(rows, axis=0), b - r)
+            return sums
+
+        total[step, pl.ds(0, r), :] = summed(spread(0, 1, 0), 1)
+        total[step, pl.ds(r + p.rows, r), :] = summed(spread(2, 1, 1), 1)
+        edges = copies(2 * step + 1, total.at[step, pl.ds(0, r)], total.at[step, pl.ds(r + p.rows, r)],
+                       got.at[step, 0, pl.ds(r, r)], got.at[step, 1, pl.ds(0, r)])
+        start(edges)
+        own = summed(spread(1, 2, 0) + spread(0, 2, 1), 2)
         if step < ITERS - 1:
-            pair = copies(step + 1, total.at[step, pl.ds(0, half)], total.at[step, pl.ds(half, half)],
-                          got.at[step, 0], got.at[step, 1])
+            total[step, pl.ds(r, p.rows), :] = own
+            pair = copies(2 * step + 2, total.at[step, pl.ds(r, r)], total.at[step, pl.ds(p.rows, r)],
+                          got.at[step, 0, pl.ds(0, r)], got.at[step, 1, pl.ds(r, r)])
             start(pair)
+            finish(edges)
             finish(pair)
-            gradient = sums + jnp.concatenate([got[step, 0], got[step, 1]], axis=0)
+            gradient = total[step] + jnp.concatenate([got[step, 0], got[step, 1]], axis=0)
             after = field[...] - STEP_RATE * gradient
             row = lax.broadcasted_iota(jnp.int32, after.shape, 0)
-            inside = ((row >= r) | has_up) & ((row < p.ext - r) | has_down)
-            field[...] = jnp.where(inside, after, 0.0)
+            kept = ((row >= r) | has_up) & ((row < p.ext - r) | has_down)
+            field[...] = jnp.where(kept, after, 0.0)
         else:
-            pair = copies(step + 1, total.at[step, pl.ds(0, r)], total.at[step, pl.ds(p.ext - r, r)],
-                          got.at[step, 0, pl.ds(half - r, r)], got.at[step, 1, pl.ds(0, r)])
-            start(pair)
-            finish(pair)
-            outer = jnp.concatenate([got[step, 0, pl.ds(half - r, r)], got[step, 1, pl.ds(0, r)]], axis=0)
-            own = sums[r : r + p.rows]
-            out_ref[...] = field[pl.ds(r, p.rows), :] - STEP_RATE * (own + outer)
-
-
-def laid_out(kernels, p):
-    corners, channels, side, _ = kernels.shape
-    value = jnp.swapaxes(kernels, 2, 3).astype(jnp.float32)
-    value = jnp.pad(value, ((0, 0), (0, 0), (0, p.stretches * p.per - side), (0, p.window - side)))
-    value = value.reshape(corners, channels, p.stretches, p.per * p.window)
-    value = jnp.pad(value, ((0, 0), (0, 0), (0, 0), (0, LANES - p.per * p.window)))
-    return value.reshape(corners, channels, p.depth)
+            before = field[pl.ds(r, p.rows), :]
+            finish(edges)
+            outer = jnp.concatenate([got[step, 0, pl.ds(r, r)], got[step, 1, pl.ds(0, r)]], axis=0)
+            out_ref[...] = before - STEP_RATE * (own + outer)
 
 
 def body(devices, mask, target, kernels, corner_weights, hotspots, counts):
     rows, width = mask.shape
     p = Plan(rows, width, kernels.shape[1], kernels.shape[-1], hotspots.shape[1])
     assert rows == 2 * p.radius and p.radius == 8
-    base = laid_out(kernels, p)
+    taps = jnp.transpose(kernels, (0, 2, 1, 3))
     smem = pl.BlockSpec(memory_space=pltpu.SMEM)
     vmem = pl.BlockSpec(memory_space=pltpu.VMEM)
     wide = p.groups * width
     return pl.pallas_call(
         functools.partial(kernel, p, devices),
         out_shape=jax.ShapeDtypeStruct((rows, width), jnp.float32),
-        in_specs=[smem, smem, smem, vmem, vmem, vmem],
+        in_specs=[smem, smem, smem, vmem, vmem, pl.BlockSpec(memory_space=pl.ANY)],
         out_specs=vmem,
         scratch_shapes=[
+            pltpu.VMEM(taps.shape, taps.dtype),
+            pltpu.VMEM((p.slots * p.channels, p.packed), jnp.float32),
             pltpu.VMEM((p.mix, p.depth), jnp.float32),
-            pltpu.VMEM((p.depth, p.mix), jnp.bfloat16),
+            pltpu.VMEM((p.slots * p.slot_rows, p.depth), jnp.bfloat16),
+            pltpu.VMEM((p.window // p.radius * p.block, p.mix), jnp.bfloat16),
             pltpu.VMEM((p.depth, wide), jnp.bfloat16),
             pltpu.VMEM((p.mix, wide), jnp.bfloat16),
             pltpu.VMEM((p.ext, width), jnp.float32),
             pltpu.VMEM((ITERS, p.ext, width), jnp.float32),
             pltpu.VMEM((2, p.radius, width), jnp.float32),
             pltpu.VMEM((ITERS, 2, p.ext // 2, width), jnp.float32),
-            pltpu.SemaphoreType.DMA((ITERS + 1, 2)),
-            pltpu.SemaphoreType.DMA((ITERS + 1, 2)),
+            pltpu.SemaphoreType.DMA,
+            pltpu.SemaphoreType.DMA((2 * ITERS, 2)),
+            pltpu.SemaphoreType.DMA((2 * ITERS, 2)),
         ],
         compiler_params=pltpu.CompilerParams(collective_id=0, has_side_effects=True),
         name="litho",
-    )(hotspots, counts, corner_weights, mask, target, base)
+    )(hotspots.T, counts, corner_weights, mask, target, taps)
 
 
 def solution(mesh):

time: 21.7 us -> 16.2 us (0.75)
  local copies, waits for them, and re-layouts: 7.38 us -> 1.32 us
  Pallas kernels: 13.9 us -> 14.6 us
    unnamed x5 -> x1, local copies, waits for them, and re-layouts: 5.4 us -> 1.32 us
    reshape x2 -> x0, local copies, waits for them, and re-layouts: 1.67 us -> none  [the longest x1 0.94 us: laid_out(): return value.reshape(corners, channels, p.depth)]
    pallas_call x1, Pallas kernels: 13.9 us -> 14.6 us  [body(): pl.pallas_call(functools.partial(kernel, p, devices), out_shape=jax.Shape...]
    pad x1 -> x0, local copies, waits for them, and re-layouts: 0.31 us -> none  [laid_out(): jnp.pad(value, ((0, 0), (0, 0), (0, p.stretches * p.per - side), (0, p.wi...]
where the time goes in v1:
time: 16.2 us; the launch traced here: 15.9 us
  Pallas kernels  14.6 us (90%)
  local copies, waits for them, and re-layouts  1.32 us (8%)
    pallas_call x1, Pallas kernels, body(): pl.pallas_call(functools.partial(kernel, p, devices), out_shape=jax.Shape...  14.6 us
    unnamed x1, local copies, waits for them, and re-layouts  1.32 us

profile of v1, /device:TPU:7, one launch (start us, length us, event | category | flops | bytes accessed | tf_op | source)
XLA Modules:
  0.0 15.9 jit_solution(12760910395705607998)
XLA Ops:
  0.0 14.6 %litho.1 = f32[16,256]{1,0:T(8,128)} custom-call(s32[5,16]{1,0:T(8,128)} %bitcast.3, s32[16]{0:T(128)} %count_ref.1, f32[9,12]{1,0:T(8,128)} %weight_ref.1, f32[16,256]{1,0:T(8,128)} %mask_ref.1, f32[16,256]{1,0:T(8,128)} %target_ref.1, bf16[9,17,24,17]{3,2,1,0:T(8,128)(2,1)} %bitcast.2), custom_call_target="tpu_custom_call" | custom-call | tf_op jit(solution)/shard_map/litho/pallas_call | solution.py:261
  14.6 1.3 %copy.8 = f32[16,256]{1,0:T(8,128)} copy(f32[16,256]{1,0:T(8,128)} %litho.1) | data formatting | bytes 32768

commit v2 on v1

--- a/solution.py
+++ b/solution.py
@@ -54,16 +54,14 @@
     return jnp.where(keep, moved, 0.0)
 
 
-def kernel(p, devices, hot_ref, count_ref, weight_ref, mask_ref, target_ref, taps_hbm, out_ref,
-           taps, pack, big, big_low, big_t, patches, source, field, total, halo, got,
-           load_sem, send_sem, recv_sem):
+def kernel(p, devices, hot_hbm, count_hbm, weight_hbm, mask_hbm, target_hbm, taps_hbm, out_ref,
+           hot_ref, count_ref, weight_ref, target_ref, taps, pack, big, big_low, big_t, patches,
+           source, field, total, got, load_sem, send_sem, recv_sem):
     me = lax.axis_index("row")
     r = p.radius
     has_up, has_down = me > 0, me < devices - 1
-    kinds = weight_ref.shape[1]
-
-    load = pltpu.make_async_copy(taps_hbm, taps, load_sem)
-    load.start()
+    kinds = weight_hbm.shape[1]
+
     barrier = pltpu.get_barrier_semaphore()
 
     @pl.when(has_up)
@@ -73,6 +71,12 @@
     @pl.when(has_down)
     def _():
         pl.semaphore_signal(barrier, inc=1, device_id={"row": me + 1}, device_id_type=MESH)
+
+    pairs = ((taps_hbm, taps), (hot_hbm, hot_ref), (count_hbm, count_ref), (weight_hbm, weight_ref),
+             (target_hbm, target_ref), (mask_hbm, field.at[pl.ds(r, p.rows)]))
+    loads = [pltpu.make_async_copy(a, b, load_sem.at[k]) for k, (a, b) in enumerate(pairs)]
+    for load in loads:
+        load.start()
 
     def copies(stage, up_src, down_src, above, below):
         up = pltpu.make_async_remote_copy(
@@ -109,13 +113,13 @@
 
     @pl.when(jnp.logical_not(has_up))
     def _():
-        halo[0] = jnp.zeros(halo.shape[1:], halo.dtype)
+        field[pl.ds(0, r), :] = jnp.zeros((r, p.width), field.dtype)
         for step in range(ITERS):
             got[step, 0] = jnp.zeros(got.shape[2:], got.dtype)
 
     @pl.when(jnp.logical_not(has_down))
     def _():
-        halo[1] = jnp.zeros(halo.shape[1:], halo.dtype)
+        field[pl.ds(r + p.rows, r), :] = jnp.zeros((r, p.width), field.dtype)
         for step in range(ITERS):
             got[step, 1] = jnp.zeros(got.shape[2:], got.dtype)
 
@@ -131,28 +135,29 @@
     wanted = jnp.where(valid, tap_row * p.lane_step + tap_col, -1)
     place = (lax.broadcasted_iota(jnp.int32, shape, 0) == wanted).astype(jnp.float32).astype(jnp.bfloat16)
 
+    pack[...] = jnp.zeros(pack.shape, jnp.float32)
+    inner = has_up & has_down
+
+    @pl.when(inner)
+    def _():
+        pl.semaphore_wait(barrier, 2)
+
+    @pl.when(jnp.logical_not(inner))
+    def _():
+        pl.semaphore_wait(barrier, 1)
+
+    first = copies(0, mask_hbm.at[pl.ds(0, r)], mask_hbm.at[pl.ds(p.rows - r, r)],
+                   field.at[pl.ds(0, r)], field.at[pl.ds(r + p.rows, r)])
+    start(first)
+
+    for load in loads:
+        load.wait()
     corners = [hot_ref[s, me] for s in range(p.slots)]
     count = count_ref[me]
-    pack[...] = jnp.zeros(pack.shape, jnp.float32)
-    load.wait()
     for s in range(p.slots):
         for a in range(p.side):
             pack[pl.ds(s * p.channels, p.channels), pl.ds(a * p.lane_step, p.side)] = (
                 taps[corners[s], a].astype(jnp.float32))
-
-    inner = has_up & has_down
-
-    @pl.when(inner)
-    def _():
-        pl.semaphore_wait(barrier, 2)
-
-    @pl.when(jnp.logical_not(inner))
-    def _():
-        pl.semaphore_wait(barrier, 1)
-
-    first = copies(0, mask_ref.at[pl.ds(0, r)], mask_ref.at[pl.ds(p.rows - r, r)],
-                   halo.at[0], halo.at[1])
-    start(first)
 
     base = jnp.dot(pack[...].astype(jnp.bfloat16), place, preferred_element_type=jnp.float32)
     for s in range(p.slots):
@@ -182,9 +187,6 @@
 
     target = jnp.concatenate([target_ref[pl.ds(g * r, r), :] for g in range(p.groups)], axis=1)
     finish(first)
-    field[pl.ds(0, r), :] = halo[0]
-    field[pl.ds(r, p.rows), :] = mask_ref[...]
-    field[pl.ds(r + p.rows, r), :] = halo[1]
 
     for step in range(ITERS):
         low = field[...].astype(jnp.bfloat16).astype(jnp.float32)
@@ -255,15 +257,18 @@
     p = Plan(rows, width, kernels.shape[1], kernels.shape[-1], hotspots.shape[1])
     assert rows == 2 * p.radius and p.radius == 8
     taps = jnp.transpose(kernels, (0, 2, 1, 3))
-    smem = pl.BlockSpec(memory_space=pltpu.SMEM)
     vmem = pl.BlockSpec(memory_space=pltpu.VMEM)
     wide = p.groups * width
     return pl.pallas_call(
         functools.partial(kernel, p, devices),
-        out_shape=jax.ShapeDtypeStruct((rows, width), jnp.float32),
-        in_specs=[smem, smem, smem, vmem, vmem, pl.BlockSpec(memory_space=pl.ANY)],
+        out_shape=pltpu.VMEM((rows, width), jnp.float32),
+        in_specs=[pl.BlockSpec(memory_space=pl.ANY)] * 6,
         out_specs=vmem,
         scratch_shapes=[
+            pltpu.SMEM(hotspots.shape[::-1], hotspots.dtype),
+            pltpu.SMEM(counts.shape, counts.dtype),
+            pltpu.SMEM(corner_weights.shape, corner_weights.dtype),
+            pltpu.VMEM(target.shape, target.dtype),
             pltpu.VMEM(taps.shape, taps.dtype),
             pltpu.VMEM((p.slots * p.channels, p.packed), jnp.float32),
             pltpu.VMEM((p.mix, p.depth), jnp.float32),
@@ -273,9 +278,8 @@
             pltpu.VMEM((p.mix, wide), jnp.bfloat16),
             pltpu.VMEM((p.ext, width), jnp.float32),
             pltpu.VMEM((ITERS, p.ext, width), jnp.float32),
-            pltpu.VMEM((2, p.radius, width), jnp.float32),
             pltpu.VMEM((ITERS, 2, p.ext // 2, width), jnp.float32),
-            pltpu.SemaphoreType.DMA,
+            pltpu.SemaphoreType.DMA((6,)),
             pltpu.SemaphoreType.DMA((2 * ITERS, 2)),
             pltpu.SemaphoreType.DMA((2 * ITERS, 2)),
         ],

time: 16.2 us -> 13.6 us (0.84)
  Pallas kernels: 14.6 us -> 12.8 us
  local copies, waits for them, and re-layouts: 1.32 us -> 0.61 us
    pallas_call x1, Pallas kernels: 14.6 us -> 12.8 us  [body(): pl.pallas_call(functools.partial(kernel, p, devices), out_shape=pltpu.VME...]
    unnamed x1, local copies, waits for them, and re-layouts: 1.32 us -> 0.61 us
where the time goes in v2:
time: 13.6 us; the launch traced here: 13.4 us
  Pallas kernels  12.8 us (94%)
  local copies, waits for them, and re-layouts  0.61 us (4%)
    pallas_call x1, Pallas kernels, body(): pl.pallas_call(functools.partial(kernel, p, devices), out_shape=pltpu.VME...  12.8 us
    unnamed x1, local copies, waits for them, and re-layouts  0.61 us

profile of v2, /device:TPU:7, one launch (start us, length us, event | category | flops | bytes accessed | tf_op | source)
XLA Modules:
  0.0 13.4 jit_solution(18327195175300831258)
XLA Ops:
  0.0 12.8 %litho.1 = f32[16,256]{1,0:T(8,128)S(1)} custom-call(s32[5,16]{1,0:T(8,128)} %bitcast.3, s32[16]{0:T(128)} %count_hbm.1, f32[9,12]{1,0:T(8,128)} %weight_hbm.1, f32[16,256]{1,0:T(8,128)} %mask_hbm.1, f32[16,256]{1,0:T(8,128)} %target_hbm.1, bf16[9,17,24,17]{3,2,1,0:T(8,128)(2,1)} %bitcast.2), custom_call_target="tpu_custom_call" | custom-call | tf_op jit(solution)/shard_map/litho/pallas_call | solution.py:262
  12.8 0.6 %copy.8 = f32[16,256]{1,0:T(8,128)} copy(f32[16,256]{1,0:T(8,128)S(1)} %litho.1) | data formatting | bytes 32768
